TPU v7x, 256 devices: a whole 4x4x8 slice. The times are simulated.
256 devices in a mesh: ctx: 32 (over y, z), ret: 2 (over core), tp: 4 (over x).
Axes of the slice: x: 4, y: 4, z: 8, core: 2. Of those that a mesh axis runs over, the one named last changes fastest.
Arguments:
- queries: bfloat16 [32768, 2048], P('ctx', 'tp'), may hold values from -256 to 256
- d_attn: bfloat16 [32768, 2048], P('ctx', 'tp'), may hold values from -6 to 6
- pool: bfloat16 [2, 32768, 896], P('ret', 'ctx'), may hold values from -6 to 6
- w_key: bfloat16 [896, 2048], P(None, 'tp'), may hold values from -0.1875 to 0.1875
- w_value: bfloat16 [896, 2048], P(None, 'tp'), may hold values from -0.1875 to 0.1875
- owners: int32 [512, 2], replicated, may hold values from 0 to 31, as said below
- picks: int32 [512, 2], replicated, may hold values from 0 to 1023
- live_counts: int32 [2, 32], replicated, may hold values from 1 to 8
Outputs:
- attn_out: bfloat16 [32768, 2048], P('ctx', 'tp')
- d_queries: bfloat16 [32768, 2048], P('ctx', 'tp')
- d_w_key: bfloat16 [896, 2048], P(None, 'tp')
- d_w_value: bfloat16 [896, 2048], P(None, 'tp')
Inputs may be any that keep to these rules, and one draw needn't show every extreme that they name: `owners`: in each column, at most 1 of the 16 spans of one ctx slab name the same owner, and in every slab some owner is named exactly 1 times.
All inputs are finite; a program needn't handle non-finite values.
Results may differ from a plain program's by a relative error of at most 0.0095.
The roundings to bfloat16 on the way count: a program that leaves them out, or rounds other values in their place, can miss the bound.
Values may be sent and summed in bfloat16 or wider, within the bound.
No kernel may reach another device: no remote copies, remote signals or barrier semaphores. Data moves between devices by JAX's collectives and lax.ppermute only.
A program may use at most 128 MiB of HBM per device.

v0:
```python
import math
import jax
import jax.numpy as jnp
from jax import lax
from jax.sharding import PartitionSpec as P

HEAD_DIM = 128
SPAN = 64
NBR_LEN = 128
CH_DEV = 16


def combined_all(x, axis, combine):
    everything = jax.tree.map(lambda part: lax.all_gather(part, axis), x)
    leading = jax.tree.map(lambda part: part[0], everything)

    def hop(k, so_far):
        return combine(so_far, jax.tree.map(lambda part: part[k], everything))

    return lax.fori_loop(1, lax.axis_size(axis), hop, leading)


def combine_stats(earlier, later):
    first_max, first_total = earlier
    second_max, second_total = later
    joint_max = jnp.maximum(first_max, second_max)
    joint_total = first_total * jnp.exp(first_max - joint_max) + second_total * jnp.exp(
        second_max - joint_max
    )
    return (joint_max, joint_total)


def body(queries, d_attn, pool, w_key, w_value, owners, picks, live_counts):
    ctx_count = lax.axis_size("ctx")
    ctx_place = lax.axis_index("ctx")
    ret_place = lax.axis_index("ret")
    capacity = (CH_DEV + ctx_count - 1) // ctx_count
    head_cols = w_key.shape[1]
    local_heads = head_cols // HEAD_DIM
    blocks = pool.shape[1] // NBR_LEN
    enc_width = pool.shape[2]
    score_scale = 1.0 / math.sqrt(HEAD_DIM)
    owner_col = lax.dynamic_index_in_dim(owners, ret_place, 1, keepdims=False)
    pick_col = lax.dynamic_index_in_dim(picks, ret_place, 1, keepdims=False)
    count_row = lax.dynamic_index_in_dim(live_counts, ret_place, 0, keepdims=False)
    owner_ids = jnp.arange(ctx_count, dtype=jnp.int32)
    counts_of = jnp.sum(
        jnp.where(owner_col[:, None] == owner_ids[None, :], count_row[None, :], 0), axis=1
    )
    slot_col = pick_col % counts_of
    owner_grid = owner_col.reshape(ctx_count, CH_DEV)
    slot_grid = slot_col.reshape(ctx_count, CH_DEV)
    position = jnp.arange(CH_DEV, dtype=jnp.int32)
    earlier = position[None, :] < position[:, None]
    same_owner = owner_grid[:, :, None] == owner_grid[:, None, :]
    request_rank = jnp.sum(jnp.logical_and(same_owner, earlier[None]), axis=2)
    places = jnp.arange(capacity, dtype=jnp.int32)
    wanted = jnp.logical_and(
        (owner_grid == ctx_place)[:, None, :], request_rank[:, None, :] == places[None, :, None]
    )
    send_slot = jnp.sum(jnp.where(wanted, slot_grid[:, None, :], 0), axis=2).reshape(-1)
    send_live = jnp.any(wanted, axis=2).reshape(-1)
    my_owner = lax.dynamic_index_in_dim(owner_grid, ctx_place, 0, keepdims=False)
    my_rank = lax.dynamic_index_in_dim(request_rank, ctx_place, 0, keepdims=False)
    recv_index = my_owner * capacity + my_rank
    pool_blocks = pool[0].reshape(blocks, NBR_LEN, enc_width)
    flat_pool = pool[0]
    own_keys = jnp.dot(flat_pool, w_key, preferred_element_type=jnp.float32).astype(jnp.bfloat16)
    own_values = jnp.dot(flat_pool, w_value, preferred_element_type=jnp.float32).astype(
        jnp.bfloat16
    )
    own_pair = jnp.concatenate([own_keys, own_values], axis=1).reshape(
        blocks, NBR_LEN, 2 * head_cols
    )
    outgoing = jnp.take(own_pair, send_slot, axis=0)
    incoming = lax.all_to_all(outgoing, "ctx", split_axis=0, concat_axis=0, tiled=True)
    chosen = jnp.take(incoming, recv_index, axis=0)
    key_tiles = chosen[:, :, :head_cols]
    value_tiles = chosen[:, :, head_cols:]
    query_tiles = queries.reshape(CH_DEV, SPAN, local_heads, HEAD_DIM)
    grad_out = d_attn.reshape(CH_DEV, SPAN, local_heads, HEAD_DIM)
    key_four = key_tiles.reshape(CH_DEV, NBR_LEN, local_heads, HEAD_DIM)
    value_four = value_tiles.reshape(CH_DEV, NBR_LEN, local_heads, HEAD_DIM)
    scores = (
        jnp.einsum("cmhd,clhd->chml", query_tiles, key_four, preferred_element_type=jnp.float32)
        * score_scale
    )
    local_max = jnp.max(scores, axis=3)
    local_total = jnp.sum(jnp.exp(scores - local_max[..., None]), axis=3)
    row_max, row_total = combined_all((local_max, local_total), "ret", combine_stats)
    attn_prob = jnp.exp(scores - row_max[..., None]) / row_total[..., None]
    prob_bf = attn_prob.astype(jnp.bfloat16)
    partial_value = jnp.einsum(
        "chml,clhd->cmhd", prob_bf, value_four, preferred_element_type=jnp.float32
    )
    attn_full = lax.psum(partial_value.reshape(CH_DEV * SPAN, head_cols), "ret")
    attn_out = attn_full.astype(jnp.bfloat16)
    out_dot = jnp.sum(
        grad_out.astype(jnp.float32)
        * attn_out.reshape(CH_DEV, SPAN, local_heads, HEAD_DIM).astype(jnp.float32),
        axis=3,
    )
    out_dot = jnp.transpose(out_dot, (0, 2, 1))
    grad_prob = jnp.einsum(
        "cmhd,clhd->chml", grad_out, value_four, preferred_element_type=jnp.float32
    )
    dscore = (attn_prob * (grad_prob - out_dot[..., None]) * score_scale).astype(jnp.bfloat16)
    dq_part = jnp.einsum("chml,clhd->cmhd", dscore, key_four, preferred_element_type=jnp.float32)
    d_queries = lax.psum(dq_part.reshape(CH_DEV * SPAN, head_cols), "ret").astype(jnp.bfloat16)
    key_grad = jnp.einsum(
        "chml,cmhd->clhd", dscore, query_tiles, preferred_element_type=jnp.float32
    ).astype(jnp.bfloat16)
    value_grad = jnp.einsum(
        "chml,cmhd->clhd", prob_bf, grad_out, preferred_element_type=jnp.float32
    ).astype(jnp.bfloat16)
    grad_pair = jnp.concatenate(
        [
            key_grad.reshape(CH_DEV, NBR_LEN, head_cols),
            value_grad.reshape(CH_DEV, NBR_LEN, head_cols),
        ],
        axis=2,
    )
    mean_share = 1.0 / (CH_DEV * ctx_count)
    back_hit = recv_index[None, :] == jnp.arange(ctx_count * capacity, dtype=jnp.int32)[:, None]
    back_span = jnp.sum(jnp.where(back_hit, position[None, :], 0), axis=1)
    returning = jnp.take(grad_pair, back_span, axis=0)
    arrived = lax.all_to_all(returning, "ctx", split_axis=0, concat_axis=0, tiled=True)
    arrived = arrived * send_live[:, None, None].astype(jnp.bfloat16)
    source = jnp.take(pool_blocks, send_slot, axis=0).reshape(-1, enc_width)
    weight_part = (
        jnp.einsum(
            "re,rk->ek",
            source,
            arrived.reshape(-1, 2 * head_cols),
            preferred_element_type=jnp.float32,
        )
        * mean_share
    )
    weight_sum = lax.psum(weight_part, ("ctx", "ret"))
    d_w_key = weight_sum[:, :head_cols].astype(jnp.bfloat16)
    d_w_value = weight_sum[:, head_cols:].astype(jnp.bfloat16)
    return (attn_out, d_queries, d_w_key, d_w_value)


def solution(mesh):
    return jax.shard_map(
        body,
        mesh=mesh,
        in_specs=(
            P("ctx", "tp"),
            P("ctx", "tp"),
            P("ret", "ctx", None),
            P(None, "tp"),
            P(None, "tp"),
            P(),
            P(),
            P(),
        ),
        out_specs=(P("ctx", "tp"), P("ctx", "tp"), P(None, "tp"), P(None, "tp")),
        check_vma=False,
    )
```

profile of v0, /device:TPU:2, one launch (start us, length us, event | category | flops | bytes accessed | tf_op | source)
XLA Modules:
  0.0 822.3 jit_solution(8104515446239602236)
XLA Ops:
  0.6 0.0 copy-start
  0.7 0.8 fusion.36
  1.5 0.7 dynamic-slice_reduce_fusion
  2.2 0.5 broadcast.249
  2.7 1.4 fusion.44
  4.1 0.1 eq.121
  4.2 0.1 copy.76
  4.3 0.1 select_reduce_fusion
  4.3 0.1 reduce_sum.62
  4.4 0.1 copy.77
  4.5 0.1 reshape.285
  4.6 0.1 copy.73
  4.6 0.1 convert_reduce_fusion
  4.8 0.2 add_reduce_fusion
  5.0 0.1 select_reduce_fusion.1
  5.1 0.1 squeeze.27
  5.2 0.1 copy.79
  5.2 0.2 fusion.35
  5.4 0.0 copy-start.6
  5.5 2.5 fusion.20
  8.0 1.3 fusion.23
  9.3 1.5 pad_maximum_fusion.1
  10.8 4.0 copy.102
  14.8 6.5 gather_fusion
  21.3 7.5 broadcast_select_fusion.1
  28.8 11.7 %all-to-all-start = ((bf16[32,128,1024]{2,1,0:T(8,128)(2,1)}), bf16[32,128,1024]{2,1,0:T(8,128)(2,1)}, u32[]{:S(2)}, u32[]{:S(2)}) async-start(bf16[32,128,1024]{2,1,0:T(8,128)(2,1)} %broadcast_select_fusion.1), calls=%async_computation | async-start | bytes 16777216 | tf_op jit(solution)/shard_map/all_to_all | solution.py:76
  40.5 1.1 reshape.291
  41.6 1.3 reshape.289
  43.0 184.8 %all-to-all-done = bf16[32,128,1024]{2,1,0:T(8,128)(2,1)} async-done(((bf16[32,128,1024]{2,1,0:T(8,128)(2,1)}), bf16[32,128,1024]{2,1,0:T(8,128)(2,1)}, u32[]{:S(2)}, u32[]{:S(2)}) %all-to-all-start) | async-done | bytes 8388640 | tf_op jit(solution)/shard_map/all_to_all | solution.py:76
  227.8 6.2 gather_fusion.1
  234.0 2.6 broadcast_select_fusion.2
  236.6 2.5 fusion.45
  239.2 4.0 copy.82
  243.1 3.9 copy.81
  247.1 2.4 bitcast_reduce_fusion
  249.5 0.0 copy-start.2
  249.5 2.0 all-gather
  251.4 1.3 fusion.15
  252.8 2.0 all-gather.1
  254.9 3.1 convolution_convert_fusion
  258.0 3.9 copy.95
  261.9 3.0 convolution_bitcast_fusion.1
  264.9 1.4 copy.86
  266.3 1.5 copy.118
  267.8 9.9 %all-reduce.3 = bf16[1024,512]{1,0:T(8,128)(2,1)} all-reduce(f32[1024,512]{1,0:T(8,128)} %bitcast.94), channel_id=1, replica_groups=mesh['ctx'=32,'ret'=2,'tp'=4] {'ret'}, use_global_device_ids=true, to_apply=%region_5.6 | all-reduce | flops 524288 | bytes 3145728 | tf_op jit(solution)/shard_map/psum | solution.py:96
  277.7 2.7 reshape.295
  280.5 3.0 multiply_reduce_fusion
  283.5 0.2 copy.89
  283.7 4.0 fusion.11
  287.7 2.1 convolution_convert_fusion.1
  289.8 3.9 copy.94
  293.8 4.8 pad_maximum_fusion
  298.5 7.1 gather_fusion.3
  305.6 7.5 broadcast_select_fusion
  313.1 13.5 %all-to-all-start.1 = ((bf16[32,128,1024]{2,1,0:T(8,128)(2,1)}), bf16[32,128,1024]{2,1,0:T(8,128)(2,1)}, u32[]{:S(2)}, u32[]{:S(2)}) async-start(bf16[32,128,1024]{2,1,0:T(8,128)(2,1)} %broadcast_select_fusion), calls=%async_computation.1 | async-start | bytes 16777216 | tf_op jit(solution)/shard_map/all_to_all | solution.py:127
  326.6 4.4 gather_fusion.2
  330.9 3.1 convolution_bitcast_fusion
  334.1 1.4 copy.91
  335.5 1.6 copy.117
  337.0 9.9 %all-reduce.4 = bf16[1024,512]{1,0:T(8,128)(2,1)} all-reduce(f32[1024,512]{1,0:T(8,128)} %bitcast.97), channel_id=1, replica_groups=mesh['ctx'=32,'ret'=2,'tp'=4] {'ret'}, use_global_device_ids=true, to_apply=%region_7.8 | all-reduce | flops 524288 | bytes 3145728 | tf_op jit(solution)/shard_map/psum | solution.py:109
  346.9 169.6 %all-to-all-done.1 = bf16[32,128,1024]{2,1,0:T(8,128)(2,1)} async-done(((bf16[32,128,1024]{2,1,0:T(8,128)(2,1)}), bf16[32,128,1024]{2,1,0:T(8,128)(2,1)}, u32[]{:S(2)}, u32[]{:S(2)}) %all-to-all-start.1) | async-done | bytes 8388640 | tf_op jit(solution)/shard_map/all_to_all | solution.py:127
  516.5 13.8 %bitcast_multiply_fusion = f32[896,1024]{1,0:T(8,128)} fusion(bf16[32,128,1024]{2,1,0:T(8,128)(2,1)} %all-to-all-done.1, bf16[32]{0:T(256)(128)(2,1)S(1)} %convert_element_type.66, bf16[32,128,896]{2,1,0:T(8,128)(2,1)} %gather_fusion.2, pred[32]{0:T(512)(128)(4,1)S(1)} %get-tuple-element.35), kind=kOutput, calls=%fused_computation.13 | convolution fusion | flops 7524974592 | bytes 19398752 | tf_op jit(solution)/shard_map/re,rk->ek/dot_general | solution.py:131
  530.3 289.2 %all-reduce.5 = bf16[896,1024]{1,0:T(8,128)(2,1)} all-reduce(f32[896,1024]{1,0:T(8,128)} %bitcast_multiply_fusion), channel_id=1, replica_groups=mesh['ctx'=32,'ret'=2,'tp'=4] {'ctx','ret'}, use_global_device_ids=true, to_apply=%region_10.11 | all-reduce | flops 917504 | bytes 5505024 | tf_op jit(solution)/shard_map/psum | solution.py:139
  819.5 2.8 fusion.46
  (23 shorter events, 0.2 us)
Async XLA Ops:
  0.6 4.8 copy-start
  5.4 2.6 copy-start.6
  28.7 11.7 %copy-start.5 = (bf16[1024,512]{1,0:T(8,128)(2,1)S(1)}, bf16[1024,512]{1,0:T(8,128)(2,1)}, u32[]{:S(2)}) copy-start(bf16[1024,512]{1,0:T(8,128)(2,1)} %param.9) | copy-start | bytes 3145732
  28.8 199.1 %all-to-all-start = ((bf16[32,128,1024]{2,1,0:T(8,128)(2,1)}), bf16[32,128,1024]{2,1,0:T(8,128)(2,1)}, u32[]{:S(2)}, u32[]{:S(2)}) async-start(bf16[32,128,1024]{2,1,0:T(8,128)(2,1)} %broadcast_select_fusion.1), calls=%async_computation | async-start | bytes 16777216 | tf_op jit(solution)/shard_map/all_to_all | solution.py:76
  249.4 8.5 %copy-start.1 = (f32[16,4,128,64]{2,3,1,0:T(8,128)}, f32[16,4,128,64]{2,3,1,0:T(8,128)S(1)}, u32[]{:S(2)}) copy-start(f32[16,4,128,64]{2,3,1,0:T(8,128)S(1)} %get-tuple-element.33) | copy-start | bytes 6291460
  249.5 5.4 copy-start.2
  287.7 2.1 copy-start.3
  313.1 203.5 %all-to-all-start.1 = ((bf16[32,128,1024]{2,1,0:T(8,128)(2,1)}), bf16[32,128,1024]{2,1,0:T(8,128)(2,1)}, u32[]{:S(2)}, u32[]{:S(2)}) async-start(bf16[32,128,1024]{2,1,0:T(8,128)(2,1)} %broadcast_select_fusion), calls=%async_computation.1 | async-start | bytes 16777216 | tf_op jit(solution)/shard_map/all_to_all | solution.py:127
  326.6 4.4 copy-start.4
where the time goes:
time: 823 us; the launch traced here: 822 us
  waiting for transfers between devices  354 us (43%)
  blocking collectives  313 us (38%)
  local copies, waits for them, and re-layouts  64.5 us (8%)
  matrix products  35.3 us (4%)
  other arithmetic  28.9 us (4%)
  starting transfers between devices  25.2 us (3%)
    psum x1, blocking collectives, body(): weight_sum = lax.psum(weight_part, ('ctx', 'ret'))  289 us
    all_to_all x1, waiting for transfers between devices, body(): lax.all_to_all(outgoing, 'ctx', split_axis=0, concat_axis=0, tiled=True)  185 us
    all_to_all x1, waiting for transfers between devices, body(): lax.all_to_all(returning, 'ctx', split_axis=0, concat_axis=0, tiled=True)  170 us
  transfers between devices with their start and end apart: 2, of which 2 were waited for; matrix products, arithmetic and copies ran while one was open for 2% of the time, Pallas kernels for 0%

commit v1 on v0

--- a/solution.py
+++ b/solution.py
@@ -136,7 +136,7 @@
         )
         * mean_share
     )
-    weight_sum = lax.psum(weight_part, ("ctx", "ret"))
+    weight_sum = lax.psum(lax.psum(weight_part, axis_name="ret"), axis_name="ctx")
     d_w_key = weight_sum[:, :head_cols].astype(jnp.bfloat16)
     d_w_value = weight_sum[:, head_cols:].astype(jnp.bfloat16)
     return (attn_out, d_queries, d_w_key, d_w_value)

time: 823 us -> 765 us (0.930)
  blocking collectives: 313 us -> 201 us
  waiting for transfers between devices: 354 us -> 393 us
  between operations: 0.92 us -> 14.3 us
    psum x1, blocking collectives: 289 us -> 177 us  [body(): lax.psum(lax.psum(weight_part, axis_name='ret'), axis_name='ctx')]
    psum x0 -> x1, waiting for transfers between devices: none -> 22.4 us  [body(): lax.psum(weight_part, axis_name='ret')]
    all_to_all x1, waiting for transfers between devices: 170 us -> 186 us  [body(): lax.all_to_all(returning, 'ctx', split_axis=0, concat_axis=0, tiled=True)]
  transfers between devices with their start and end apart: 2 -> 3, of which waited for: 2 -> 3; matrix products, arithmetic and copies ran while one was open for 2% -> 2% of each run, Pallas kernels for 0% -> 0%
where the time goes in v1:
time: 765 us; the launch traced here: 764 us
  waiting for transfers between devices  393 us (51%)
  blocking collectives  201 us (26%)
  local copies, waits for them, and re-layouts  65.6 us (9%)
  matrix products  35.3 us (5%)
  other arithmetic  28.9 us (4%)
  starting transfers between devices  25.3 us (3%)
  between operations  14.3 us (2%)
    all_to_all x1, waiting for transfers between devices, body(): lax.all_to_all(returning, 'ctx', split_axis=0, concat_axis=0, tiled=True)  186 us
    all_to_all x1, waiting for transfers between devices, body(): lax.all_to_all(outgoing, 'ctx', split_axis=0, concat_axis=0, tiled=True)  185 us
    psum x1, blocking collectives, body(): lax.psum(lax.psum(weight_part, axis_name='ret'), axis_name='ctx')  177 us
    psum x1, waiting for transfers between devices, body(): lax.psum(weight_part, axis_name='ret')  22.4 us
  transfers between devices with their start and end apart: 3, of which 3 were waited for; matrix products, arithmetic and copies ran while one was open for 2% of the time, Pallas kernels for 0%

profile of v1, /device:TPU:2, one launch (start us, length us, event | category | flops | bytes accessed | tf_op | source)
XLA Modules:
  0.0 763.6 jit_solution(15549320527762230271)
XLA Ops:
  7.2 0.8 fusion.36
  8.0 0.7 dynamic-slice_reduce_fusion
  8.7 0.5 broadcast.249
  9.2 1.4 fusion.44
  10.6 0.1 eq.121
  10.7 0.1 copy.76
  10.8 0.1 select_reduce_fusion
  10.9 0.1 reduce_sum.62
  11.0 0.1 copy.77
  11.0 0.1 reshape.285
  11.1 0.1 copy.73
  11.2 0.1 convert_reduce_fusion
  11.3 0.2 add_reduce_fusion
  11.5 0.1 select_reduce_fusion.1
  11.6 0.1 squeeze.27
  11.7 0.1 copy.79
  11.8 0.2 fusion.35
  12.0 2.5 fusion.20
  14.6 1.3 fusion.23
  15.9 1.5 pad_maximum_fusion.1
  17.3 4.0 copy.102
  21.3 6.5 gather_fusion
  27.8 7.5 broadcast_select_fusion.1
  35.3 11.7 %all-to-all-start = ((bf16[32,128,1024]{2,1,0:T(8,128)(2,1)}), bf16[32,128,1024]{2,1,0:T(8,128)(2,1)}, u32[]{:S(2)}, u32[]{:S(2)}) async-start(bf16[32,128,1024]{2,1,0:T(8,128)(2,1)} %broadcast_select_fusion.1), calls=%async_computation | async-start | bytes 16777216 | tf_op jit(solution)/shard_map/all_to_all | solution.py:76
  47.0 1.1 reshape.291
  48.1 1.3 reshape.289
  49.5 184.8 %all-to-all-done = bf16[32,128,1024]{2,1,0:T(8,128)(2,1)} async-done(((bf16[32,128,1024]{2,1,0:T(8,128)(2,1)}), bf16[32,128,1024]{2,1,0:T(8,128)(2,1)}, u32[]{:S(2)}, u32[]{:S(2)}) %all-to-all-start) | async-done | bytes 8388640 | tf_op jit(solution)/shard_map/all_to_all | solution.py:76
  234.4 6.2 gather_fusion.1
  240.5 2.6 broadcast_select_fusion.2
  243.2 2.5 fusion.45
  245.7 4.0 copy.82
  249.7 3.9 copy.81
  253.6 2.4 bitcast_reduce_fusion
  256.0 2.0 all-gather
  258.0 1.3 fusion.15
  259.3 2.0 all-gather.1
  261.4 3.1 convolution_convert_fusion
  264.5 3.9 copy.95
  268.4 3.0 convolution_bitcast_fusion.1
  271.4 1.4 copy.86
  272.9 1.5 copy.118
  274.4 9.9 %all-reduce.6 = bf16[1024,512]{1,0:T(8,128)(2,1)} all-reduce(f32[1024,512]{1,0:T(8,128)} %bitcast.94), channel_id=1, replica_groups=mesh['ctx'=32,'ret'=2,'tp'=4] {'ret'}, use_global_device_ids=true, to_apply=%region_5.6 | all-reduce | flops 524288 | bytes 3145728 | tf_op jit(solution)/shard_map/psum | solution.py:96
  284.3 2.7 reshape.295
  287.0 3.0 multiply_reduce_fusion
  290.0 0.2 copy.89
  290.2 4.0 fusion.11
  294.2 2.1 convolution_convert_fusion.1
  296.4 3.9 copy.94
  300.3 4.8 pad_maximum_fusion
  305.0 7.1 gather_fusion.3
  312.1 7.5 broadcast_select_fusion
  319.6 13.3 %all-to-all-start.1 = ((bf16[32,128,1024]{2,1,0:T(8,128)(2,1)}), bf16[32,128,1024]{2,1,0:T(8,128)(2,1)}, u32[]{:S(2)}, u32[]{:S(2)}) async-start(bf16[32,128,1024]{2,1,0:T(8,128)(2,1)} %broadcast_select_fusion), calls=%async_computation.1 | async-start | bytes 16777216 | tf_op jit(solution)/shard_map/all_to_all | solution.py:127
  332.9 0.3 all-reduce.5.cloned.1.call-start
  333.2 4.4 gather_fusion.2
  337.5 186.2 %all-to-all-done.1 = bf16[32,128,1024]{2,1,0:T(8,128)(2,1)} async-done(((bf16[32,128,1024]{2,1,0:T(8,128)(2,1)}), bf16[32,128,1024]{2,1,0:T(8,128)(2,1)}, u32[]{:S(2)}, u32[]{:S(2)}) %all-to-all-start.1) | async-done | bytes 8388640 | tf_op jit(solution)/shard_map/all_to_all | solution.py:127
  523.7 13.8 %bitcast_multiply_fusion = f32[896,1024]{1,0:T(8,128)} fusion(bf16[32,128,1024]{2,1,0:T(8,128)(2,1)} %all-to-all-done.1, bf16[32]{0:T(256)(128)(2,1)S(1)} %convert_element_type.66, bf16[32,128,896]{2,1,0:T(8,128)(2,1)} %gather_fusion.2, pred[32]{0:T(512)(128)(4,1)S(1)} %get-tuple-element.35), kind=kOutput, calls=%fused_computation.13 | convolution fusion | flops 7524974592 | bytes 19398752 | tf_op jit(solution)/shard_map/re,rk->ek/dot_general | solution.py:131
  537.5 1.2 copy-done.4
  538.7 3.1 convolution_bitcast_fusion
  541.8 1.4 copy.91
  543.2 1.5 copy.117
  544.7 9.9 %all-reduce.7 = bf16[1024,512]{1,0:T(8,128)(2,1)} all-reduce(f32[1024,512]{1,0:T(8,128)} %bitcast.97), channel_id=1, replica_groups=mesh['ctx'=32,'ret'=2,'tp'=4] {'ret'}, use_global_device_ids=true, to_apply=%region_7.8 | all-reduce | flops 524288 | bytes 3145728 | tf_op jit(solution)/shard_map/psum | solution.py:109
  554.6 22.4 %all-reduce.5.cloned.1.call-done = f32[896,1024]{1,0:T(8,128)} async-done(((f32[896,1024]{1,0:T(8,128)}), f32[896,1024]{1,0:T(8,128)}) %all-reduce.5.cloned.1.call-update) | async-done | bytes 3670032 | tf_op jit(solution)/shard_map/psum | solution.py:139
  577.0 177.0 %all-reduce.8 = bf16[896,1024]{1,0:T(8,128)(2,1)} all-reduce(f32[896,1024]{1,0:T(8,128)} %all-reduce.5.cloned.1.call-done), channel_id=1, replica_groups=mesh['ctx'=32,'ret'=2,'tp'=4] {'ctx'}, use_global_device_ids=true, to_apply=%region_11.12 | all-reduce | flops 917504 | bytes 5505024 | tf_op jit(solution)/shard_map/psum | solution.py:139
  754.0 2.8 fusion.46
  (26 shorter events, 0.2 us)
Async XLA Ops:
  7.2 4.8 copy-start
  12.0 2.6 copy-start.6
  35.3 11.7 %copy-start.5 = (bf16[1024,512]{1,0:T(8,128)(2,1)S(1)}, bf16[1024,512]{1,0:T(8,128)(2,1)}, u32[]{:S(2)}) copy-start(bf16[1024,512]{1,0:T(8,128)(2,1)} %param.9) | copy-start | bytes 3145732
  35.3 199.1 %all-to-all-start = ((bf16[32,128,1024]{2,1,0:T(8,128)(2,1)}), bf16[32,128,1024]{2,1,0:T(8,128)(2,1)}, u32[]{:S(2)}, u32[]{:S(2)}) async-start(bf16[32,128,1024]{2,1,0:T(8,128)(2,1)} %broadcast_select_fusion.1), calls=%async_computation | async-start | bytes 16777216 | tf_op jit(solution)/shard_map/all_to_all | solution.py:76
  256.0 8.5 %copy-start.1 = (f32[16,4,128,64]{2,3,1,0:T(8,128)}, f32[16,4,128,64]{2,3,1,0:T(8,128)S(1)}, u32[]{:S(2)}) copy-start(f32[16,4,128,64]{2,3,1,0:T(8,128)S(1)} %get-tuple-element.33) | copy-start | bytes 6291460
  256.0 5.4 copy-start.2
  294.2 2.1 copy-start.3
  319.6 204.1 %all-to-all-start.1 = ((bf16[32,128,1024]{2,1,0:T(8,128)(2,1)}), bf16[32,128,1024]{2,1,0:T(8,128)(2,1)}, u32[]{:S(2)}, u32[]{:S(2)}) async-start(bf16[32,128,1024]{2,1,0:T(8,128)(2,1)} %broadcast_select_fusion), calls=%async_computation.1 | async-start | bytes 16777216 | tf_op jit(solution)/shard_map/all_to_all | solution.py:127
  332.9 244.1 %all-reduce.5.cloned.1.call-start = ((), (), s32[]{:S(2)}) async-start(), calls=%async_computation.2 | async-start | bytes 7340032 | tf_op jit(solution)/shard_map/psum | solution.py:139
  537.4 1.2 copy-start.4
Sparse Core Ops, SparseCore 0:
  537.6 39.3 all-reduce.4
